TPU v7x, 32 devices: a whole 2x2x4 slice. The times are simulated.
32 devices in a mesh: groups: 2 (over x), tok: 16 (over z, y, core).
Axes of the slice: x: 2, y: 2, z: 4, core: 2. Of those that a mesh axis runs over, the one named last changes fastest.
Arguments:
- query_tokens: bfloat16 [3, 4096, 1024], P(None, ('groups', 'tok')), parts along dimension 1, may hold values from -6 to 6
- key_tokens: bfloat16 [3, 4096, 1024], P(None, ('groups', 'tok')), parts along dimension 1, may hold values from -6 to 6
- value_tokens: bfloat16 [3, 4096, 1024], P(None, ('groups', 'tok')), parts along dimension 1, may hold values from -6 to 6
- learn_rates: float32 [3, 4096, 2], P(None, ('groups', 'tok')), parts along dimension 1, may hold values from 0.0009765625 to 0.00390625
- fast_first: bfloat16 [2, 512, 512], P(None, 'tok'), may hold values from -0.25 to 0.25
- fast_third: bfloat16 [2, 512, 512], P(None, 'tok'), may hold values from -0.25 to 0.25
- fast_second: bfloat16 [2, 512, 512], P(None, 'tok'), may hold values from -0.25 to 0.25
- momentum_decay: float32 [2], replicated, may hold values from 0.3 to 0.95
Outputs:
- readout: bfloat16 [3, 4096, 1024], P(None, ('groups', 'tok')), parts along dimension 1
There are 2 independent parts, one for each index of `groups`. A program takes and returns all parts, laid end to end along the dimension named above; an argument that names none is the same for every part. Nothing has to cross between parts.
All inputs are finite; a program needn't handle non-finite values.
Results may differ from a plain program's by a relative error of at most 0.0089.
Values may be sent and summed in bfloat16 or wider, within the bound.
A program may use at most 64 MiB of HBM per device.

v0:
```python
import jax
import jax.numpy as jnp
from jax import lax
from jax.sharding import PartitionSpec as P


def forward_parts(weights, inputs):
    first, third, second = weights
    length = inputs.shape[0]
    head_count = first.shape[0]
    shaped = inputs.reshape(length, head_count, -1)
    pre_gate = jnp.einsum("thd,hfd->htf", shaped, first, preferred_element_type=jnp.float32)
    pre_up = jnp.einsum("thd,hfd->htf", shaped, third, preferred_element_type=jnp.float32)
    hidden = (jax.nn.silu(pre_gate) * pre_up).astype(jnp.bfloat16)
    return (shaped, pre_gate, pre_up, hidden)


def apply_block(weights, inputs):
    shaped, pre_gate, pre_up, hidden = forward_parts(weights, inputs)
    result = jnp.einsum("htf,hdf->thd", hidden, weights[2], preferred_element_type=jnp.float32)
    return result.reshape(inputs.shape[0], -1).astype(jnp.bfloat16)


def partial_steps(weights, keys, values, rates):
    shaped, pre_gate, pre_up, hidden = forward_parts(weights, keys)
    length = keys.shape[0]
    head_count = weights[0].shape[0]
    scaled = (
        rates[:, :, None] * values.reshape(length, head_count, -1).astype(jnp.float32)
    ).astype(jnp.bfloat16)
    step_second = jnp.einsum("thd,htf->hdf", scaled, hidden, preferred_element_type=jnp.float32)
    back = jnp.einsum("thd,hdf->htf", scaled, weights[2], preferred_element_type=jnp.float32)
    sig_gate = jax.nn.sigmoid(pre_gate)
    d_gate = (back * pre_up * sig_gate * (1.0 + pre_gate * (1.0 - sig_gate))).astype(jnp.bfloat16)
    d_up = (back * pre_gate * sig_gate).astype(jnp.bfloat16)
    step_first = jnp.einsum("htf,thd->hfd", d_gate, shaped, preferred_element_type=jnp.float32)
    step_third = jnp.einsum("htf,thd->hfd", d_up, shaped, preferred_element_type=jnp.float32)
    return (step_first, step_third, step_second)


def summed_steps(terms):
    return (
        lax.psum_scatter(terms[0], "tok", scatter_dimension=1, tiled=True),
        lax.psum_scatter(terms[1], "tok", scatter_dimension=1, tiled=True),
        lax.psum_scatter(terms[2], "tok", scatter_dimension=1, tiled=True),
    )


def renorm(old, moved):
    old_norm = jnp.sqrt(jnp.sum(old * old, axis=-1, keepdims=True) + 1e-06)
    moved_norm = jnp.sqrt(jnp.sum(moved * moved, axis=-1, keepdims=True) + 1e-06)
    return moved * old_norm / moved_norm


def full_steps(owned):
    return (
        lax.all_gather(owned[0], "tok", axis=1, tiled=True),
        lax.all_gather(owned[1], "tok", axis=1, tiled=True),
        lax.all_gather(owned[2], "tok", axis=1, tiled=True),
    )


def shards(
    query_tokens,
    key_tokens,
    value_tokens,
    learn_rates,
    fast_first,
    fast_third,
    fast_second,
    momentum_decay,
):
    full_zero = (
        lax.all_gather(fast_first, "tok", axis=1, tiled=True),
        lax.all_gather(fast_third, "tok", axis=1, tiled=True),
        lax.all_gather(fast_second, "tok", axis=1, tiled=True),
    )
    out_zero = apply_block(full_zero, query_tokens[0])
    terms_zero = partial_steps(full_zero, key_tokens[0], value_tokens[0], learn_rates[0])
    terms_one = partial_steps(full_zero, key_tokens[1], value_tokens[1], learn_rates[1])
    step_zero = summed_steps(terms_zero)
    decay = momentum_decay[:, None, None]
    weights_zero = tuple((w.astype(jnp.float32) for w in full_zero))
    whole_zero = full_steps(step_zero)
    weights_one = tuple((renorm(w, w + m) for w, m in zip(weights_zero, whole_zero)))
    full_one = tuple((w.astype(jnp.bfloat16) for w in weights_one))
    out_one = apply_block(full_one, query_tokens[1])
    step_one = summed_steps(terms_one)
    whole_one = full_steps(step_one)
    moment = tuple((decay * m + s for m, s in zip(whole_zero, whole_one)))
    weights_two = tuple((renorm(w, w + m) for w, m in zip(weights_one, moment)))
    full_two = tuple((w.astype(jnp.bfloat16) for w in weights_two))
    out_two = apply_block(full_two, query_tokens[2])
    return jnp.stack([out_zero, out_one, out_two])


def solution(mesh):
    placed = (
        P(None, ("groups", "tok"), None),
        P(None, ("groups", "tok"), None),
        P(None, ("groups", "tok"), None),
        P(None, ("groups", "tok"), None),
        P(None, "tok", None),
        P(None, "tok", None),
        P(None, "tok", None),
        P(),
    )
    return jax.shard_map(
        shards,
        mesh=mesh,
        in_specs=placed,
        out_specs=P(None, ("groups", "tok"), None),
        check_vma=False,
    )
```

profile of v0, /device:TPU:0, one launch (start us, length us, event | category | flops | bytes accessed | tf_op | source)
XLA Modules:
  0.0 798.2 jit_solution(18446105568856472642)
XLA Ops:
  10.6 39.5 %all-gather.10.cloned.1.call-done = bf16[2,512,512]{2,1,0:T(8,128)(2,1)} async-done(((bf16[2,32,512]{2,1,0:T(8,128)(2,1)}), bf16[2,512,512]{2,1,0:T(8,128)(2,1)}) %all-gather.10.cloned.1.call-update) | async-done | bytes 1048592 | tf_op jit(solution)/shard_map/all_gather | solution.py:74
  51.8 37.3 %all-gather.12.cloned.1.call-done = bf16[2,512,512]{2,1,0:T(8,128)(2,1)} async-done(((bf16[2,32,512]{2,1,0:T(8,128)(2,1)}), bf16[2,512,512]{2,1,0:T(8,128)(2,1)}) %all-gather.12.cloned.1.call-update) | async-done | bytes 1048592 | tf_op jit(solution)/shard_map/all_gather | solution.py:75
  90.9 1.9 fusion.33
  92.8 35.4 %all-gather.14.cloned.1.call-done = bf16[2,512,512]{2,1,0:T(8,128)(2,1)} async-done(((bf16[2,32,512]{2,1,0:T(8,128)(2,1)}), bf16[2,512,512]{2,1,0:T(8,128)(2,1)}) %all-gather.14.cloned.1.call-update) | async-done | bytes 1048592 | tf_op jit(solution)/shard_map/all_gather | solution.py:76
  129.8 1.9 fusion.34
  131.8 1.8 fusion.35
  136.9 1.9 fusion.36
  141.2 1.9 fusion.37
  143.2 3.1 fusion.38
  146.3 46.3 %reduce-scatter.7.cloned.1.call-done = f32[2,32,512]{2,1,0:T(8,128)} async-done(((f32[2,512,512]{2,1,0:T(8,128)}), f32[2,32,512]{2,1,0:T(8,128)}) %reduce-scatter.7.cloned.1.call-update) | async-done | bytes 131088 | tf_op jit(solution)/shard_map/reduce_scatter | solution.py:45
  192.7 64.3 %reduce-scatter.9.cloned.1.call-done = f32[2,32,512]{2,1,0:T(8,128)} async-done(((f32[2,512,512]{2,1,0:T(8,128)}), f32[2,32,512]{2,1,0:T(8,128)}) %reduce-scatter.9.cloned.1.call-update) | async-done | bytes 131088 | tf_op jit(solution)/shard_map/reduce_scatter | solution.py:43
  257.1 64.3 %reduce-scatter.11.cloned.1.call-done = f32[2,32,512]{2,1,0:T(8,128)} async-done(((f32[2,512,512]{2,1,0:T(8,128)}), f32[2,32,512]{2,1,0:T(8,128)}) %reduce-scatter.11.cloned.1.call-update) | async-done | bytes 131088 | tf_op jit(solution)/shard_map/reduce_scatter | solution.py:44
  321.4 64.5 %reduce-scatter.13.cloned.1.call-done = f32[2,32,512]{2,1,0:T(8,128)} async-done(((f32[2,512,512]{2,1,0:T(8,128)}), f32[2,32,512]{2,1,0:T(8,128)}) %reduce-scatter.13.cloned.1.call-update) | async-done | bytes 131088 | tf_op jit(solution)/shard_map/reduce_scatter | solution.py:45
  386.0 64.4 %reduce-scatter.15.cloned.1.call-done = f32[2,32,512]{2,1,0:T(8,128)} async-done(((f32[2,512,512]{2,1,0:T(8,128)}), f32[2,32,512]{2,1,0:T(8,128)}) %reduce-scatter.15.cloned.1.call-update) | async-done | bytes 131088 | tf_op jit(solution)/shard_map/reduce_scatter | solution.py:43
  450.6 64.2 %reduce-scatter.17.cloned.1.call-done = f32[2,32,512]{2,1,0:T(8,128)} async-done(((f32[2,512,512]{2,1,0:T(8,128)}), f32[2,32,512]{2,1,0:T(8,128)}) %reduce-scatter.17.cloned.1.call-update) | async-done | bytes 131088 | tf_op jit(solution)/shard_map/reduce_scatter | solution.py:44
  514.9 2.0 fusion.63
  518.0 1.8 copy.70
  519.8 1.8 copy.72
  522.9 2.6 fusion.8
  526.6 30.7 %all-gather.16.cloned.1.call-done = f32[2,512,512]{2,1,0:T(8,128)} async-done(((f32[2,32,512]{2,1,0:T(8,128)}), f32[2,512,512]{2,1,0:T(8,128)}) %all-gather.16.cloned.1.call-update) | async-done | bytes 2097168 | tf_op jit(solution)/shard_map/all_gather | solution.py:59
  557.3 2.1 fusion
  559.4 40.3 %all-gather.18.cloned.1.call-done = f32[2,512,512]{2,1,0:T(8,128)} async-done(((f32[2,32,512]{2,1,0:T(8,128)}), f32[2,512,512]{2,1,0:T(8,128)}) %all-gather.18.cloned.1.call-update) | async-done | bytes 2097168 | tf_op jit(solution)/shard_map/all_gather | solution.py:57
  599.7 2.1 fusion.1
  601.9 40.2 %all-gather.20.cloned.1.call-done = f32[2,512,512]{2,1,0:T(8,128)} async-done(((f32[2,32,512]{2,1,0:T(8,128)}), f32[2,512,512]{2,1,0:T(8,128)}) %all-gather.20.cloned.1.call-update) | async-done | bytes 2097168 | tf_op jit(solution)/shard_map/all_gather | solution.py:58
  642.0 2.1 fusion.2
  644.1 40.3 %all-gather.22.cloned.1.call-done = f32[2,512,512]{2,1,0:T(8,128)} async-done(((f32[2,32,512]{2,1,0:T(8,128)}), f32[2,512,512]{2,1,0:T(8,128)}) %all-gather.22.cloned.1.call-update) | async-done | bytes 2097168 | tf_op jit(solution)/shard_map/all_gather | solution.py:59
  684.4 42.3 %all-gather.24.cloned.1.call-done = f32[2,512,512]{2,1,0:T(8,128)} async-done(((f32[2,32,512]{2,1,0:T(8,128)}), f32[2,512,512]{2,1,0:T(8,128)}) %all-gather.24.cloned.1.call-update) | async-done | bytes 2097168 | tf_op jit(solution)/shard_map/all_gather | solution.py:57
  726.7 42.3 %all-gather.26.cloned.1.call-done = f32[2,512,512]{2,1,0:T(8,128)} async-done(((f32[2,32,512]{2,1,0:T(8,128)}), f32[2,512,512]{2,1,0:T(8,128)}) %all-gather.26.cloned.1.call-update) | async-done | bytes 2097168 | tf_op jit(solution)/shard_map/all_gather | solution.py:58
  769.0 7.4 multiply_reduce_fusion
  778.0 4.1 convolution_convert_fusion
  782.2 3.1 convolution_bitcast_fusion.3
  785.3 4.2 convolution_convert_fusion.1
  (86 shorter events, 22.6 us)
Async XLA Ops:
  6.5 3.5 copy-start.9
  6.5 43.6 %all-gather.10.cloned.1.call-start = ((), (), s32[]{:S(2)}) async-start(), calls=%async_computation.6 | async-start | bytes 1114112 | tf_op jit(solution)/shard_map/all_gather | solution.py:74
  7.3 81.9 %all-gather.12.cloned.1.call-start = ((), (), s32[]{:S(2)}) async-start(), calls=%async_computation.7 | async-start | bytes 1114112 | tf_op jit(solution)/shard_map/all_gather | solution.py:75
  8.0 120.2 %all-gather.14.cloned.1.call-start = ((), (), s32[]{:S(2)}) async-start(), calls=%async_computation.8 | async-start | bytes 1114112 | tf_op jit(solution)/shard_map/all_gather | solution.py:76
  8.7 1.9 copy-start.12
  8.8 183.9 %reduce-scatter.7.cloned.1.call-start = ((), (), s32[]{:S(2)}) async-start(), calls=%async_computation.9 | async-start | bytes 2228224 | tf_op jit(solution)/shard_map/reduce_scatter | solution.py:45
  92.8 164.2 %reduce-scatter.9.cloned.1.call-start = ((), (), s32[]{:S(2)}) async-start(), calls=%async_computation.11 | async-start | bytes 2228224 | tf_op jit(solution)/shard_map/reduce_scatter | solution.py:43
  131.7 189.6 %reduce-scatter.11.cloned.1.call-start = ((), (), s32[]{:S(2)}) async-start(), calls=%async_computation.13 | async-start | bytes 2228224 | tf_op jit(solution)/shard_map/reduce_scatter | solution.py:44
  133.6 1.5 copy-start
  133.6 2.0 copy-start.1
  133.6 252.3 %reduce-scatter.13.cloned.1.call-start = ((), (), s32[]{:S(2)}) async-start(), calls=%async_computation.15 | async-start | bytes 2228224 | tf_op jit(solution)/shard_map/reduce_scatter | solution.py:45
  135.1 1.8 copy-start.8
  135.6 0.8 copy-start.3
  136.1 0.8 copy-start.5
  136.9 2.0 copy-start.2
  138.8 311.6 %reduce-scatter.15.cloned.1.call-start = ((), (), s32[]{:S(2)}) async-start(), calls=%async_computation.17 | async-start | bytes 2228224 | tf_op jit(solution)/shard_map/reduce_scatter | solution.py:43
  138.9 2.3 copy-start.4
  138.9 2.3 copy-start.6
  140.4 0.8 copy-start.7
  143.1 371.7 %reduce-scatter.17.cloned.1.call-start = ((), (), s32[]{:S(2)}) async-start(), calls=%async_computation.19 | async-start | bytes 2228224 | tf_op jit(solution)/shard_map/reduce_scatter | solution.py:44
  146.2 411.1 %all-gather.16.cloned.1.call-start = ((), (), s32[]{:S(2)}) async-start(), calls=%async_computation.10 | async-start | bytes 2228224 | tf_op jit(solution)/shard_map/all_gather | solution.py:59
  192.7 407.1 %all-gather.18.cloned.1.call-start = ((), (), s32[]{:S(2)}) async-start(), calls=%async_computation.12 | async-start | bytes 2228224 | tf_op jit(solution)/shard_map/all_gather | solution.py:57
  257.0 385.0 %all-gather.20.cloned.1.call-start = ((), (), s32[]{:S(2)}) async-start(), calls=%async_computation.14 | async-start | bytes 2228224 | tf_op jit(solution)/shard_map/all_gather | solution.py:58
  321.4 363.1 %all-gather.22.cloned.1.call-start = ((), (), s32[]{:S(2)}) async-start(), calls=%async_computation.16 | async-start | bytes 2228224 | tf_op jit(solution)/shard_map/all_gather | solution.py:59
  385.9 340.8 %all-gather.24.cloned.1.call-start = ((), (), s32[]{:S(2)}) async-start(), calls=%async_computation.18 | async-start | bytes 2228224 | tf_op jit(solution)/shard_map/all_gather | solution.py:57
  450.4 318.6 %all-gather.26.cloned.1.call-start = ((), (), s32[]{:S(2)}) async-start(), calls=%async_computation.20 | async-start | bytes 2228224 | tf_op jit(solution)/shard_map/all_gather | solution.py:58
  601.8 167.2 %copy-start.13 = (f32[2]{0:T(128)S(1)}, f32[2]{0:T(128)}, u32[]{:S(2)}) copy-start(f32[2]{0:T(128)} %param.15) | copy-start | bytes 28
  769.0 7.6 copy-start.10
  785.3 4.2 copy-start.11
Sparse Core Ops, SparseCore 0:
  9.5 40.5 all-gather.9
  52.3 36.8 all-gather.11
  91.4 36.8 all-gather.13
  131.8 60.7 reduce-scatter.6
  196.2 60.7 reduce-scatter.8
  260.6 60.7 reduce-scatter.10
  325.1 60.7 reduce-scatter.12
  389.6 60.7 reduce-scatter.14
  454.1 60.6 reduce-scatter.16
  516.9 40.3 all-gather.15
  559.5 40.1 all-gather.17
  601.8 40.1 all-gather.19
  644.2 40.1 all-gather.21
  686.5 40.1 all-gather.23
  728.7 40.1 all-gather.25
where the time goes:
time: 799 us; the launch traced here: 798 us
  waiting for transfers between devices  719 us (90%)
  matrix products  36.7 us (5%)
  other arithmetic  14.9 us (2%)
  local copies, waits for them, and re-layouts  13.7 us (2%)
  between operations  13.6 us (2%)
    reduce_scatter x2, waiting for transfers between devices, summed_steps(): lax.psum_scatter(terms[0], 'tok', scatter_dimension=1, tiled=True)  129 us
    reduce_scatter x2, waiting for transfers between devices, summed_steps(): lax.psum_scatter(terms[1], 'tok', scatter_dimension=1, tiled=True)  128 us
    reduce_scatter x2, waiting for transfers between devices, summed_steps(): lax.psum_scatter(terms[2], 'tok', scatter_dimension=1, tiled=True)  111 us
    all_gather x2, waiting for transfers between devices, full_steps(): lax.all_gather(owned[0], 'tok', axis=1, tiled=True)  82.6 us
    all_gather x2, waiting for transfers between devices, full_steps(): lax.all_gather(owned[1], 'tok', axis=1, tiled=True)  82.4 us
    all_gather x2, waiting for transfers between devices, full_steps(): lax.all_gather(owned[2], 'tok', axis=1, tiled=True)  71 us
    all_gather x1, waiting for transfers between devices, shards(): lax.all_gather(fast_first, 'tok', axis=1, tiled=True)  39.5 us
    all_gather x1, waiting for transfers between devices, shards(): lax.all_gather(fast_third, 'tok', axis=1, tiled=True)  37.3 us
  transfers between devices with their start and end apart: 15, of which 15 were waited for; matrix products, arithmetic and copies ran while one was open for 5% of the time, Pallas kernels for 0%

commit v1 on v0

--- a/solution.py
+++ b/solution.py
@@ -2,6 +2,28 @@
 import jax.numpy as jnp
 from jax import lax
 from jax.sharding import PartitionSpec as P
+
+
+def in_order(tiles, dim):
+    tiles = jnp.moveaxis(tiles, 0, dim)
+    lengths = tiles.shape
+    return tiles.reshape(*lengths[:dim], lengths[dim] * lengths[dim + 1], *lengths[dim + 2 :])
+
+
+def collected_by_bits(x, axis):
+    count = lax.axis_size(axis)
+    blocks = x[None]
+    for level in range(count.bit_length() - 1):
+        bit = 1 << level
+        received = lax.ppermute(blocks, axis, [(i, i ^ bit) for i in range(count)])
+        both = jnp.stack([blocks, received])
+        upper = lax.axis_index(axis) >> level & 1
+        blocks = jnp.where(upper == 0, both, both[::-1]).reshape(-1, *x.shape)
+    return blocks
+
+
+def collect(x, axis, dim):
+    return in_order(collected_by_bits(x, axis), dim)
 
 
 def forward_parts(weights, inputs):
@@ -55,7 +77,7 @@
 def full_steps(owned):
     return (
         lax.all_gather(owned[0], "tok", axis=1, tiled=True),
-        lax.all_gather(owned[1], "tok", axis=1, tiled=True),
+        collect(owned[1], "tok", 1),
         lax.all_gather(owned[2], "tok", axis=1, tiled=True),
     )
 

time: 799 us -> 766 us (0.959)
  waiting for transfers between devices: 719 us -> 661 us
  other arithmetic: 14.9 us -> 28.4 us
  starting transfers between devices: 0.74 us -> 8.73 us
    all_gather x2 -> x0, waiting for transfers between devices: 82.4 us -> none  [full_steps(): lax.all_gather(owned[1], 'tok', axis=1, tiled=True)]
    ppermute x0 -> x8, waiting for transfers between devices: none -> 50.7 us  [collected_by_bits(): received = lax.ppermute(blocks, axis, [(i, i ^ bit) for i in range(count)])]
    all_gather x2, waiting for transfers between devices: 71 us -> 59.7 us  [full_steps(): lax.all_gather(owned[2], 'tok', axis=1, tiled=True)]
    another operation x0 -> x10, other arithmetic: none -> 9.87 us  [collected_by_bits(): both = jnp.stack([blocks, received])]
    ppermute x0 -> x8, starting transfers between devices: none -> 8.07 us  [collected_by_bits(): received = lax.ppermute(blocks, axis, [(i, i ^ bit) for i in range(count)])]
  transfers between devices with their start and end apart: 15 -> 21, of which waited for: 15 -> 18; matrix products, arithmetic and copies ran while one was open for 5% -> 8% of each run, Pallas kernels for 0% -> 0%
where the time goes in v1:
time: 766 us
  waiting for transfers between devices  661 us (86%)
  matrix products  35.9 us (5%)
  other arithmetic  28.4 us (4%)
  local copies, waits for them, and re-layouts  18 us (2%)
  between operations  13.8 us (2%)
  starting transfers between devices  8.73 us (1%)
    reduce_scatter x2, waiting for transfers between devices, summed_steps(): lax.psum_scatter(terms[1], 'tok', scatter_dimension=1, tiled=True)  125 us
    reduce_scatter x2, waiting for transfers between devices, summed_steps(): lax.psum_scatter(terms[0], 'tok', scatter_dimension=1, tiled=True)  121 us
    reduce_scatter x2, waiting for transfers between devices, summed_steps(): lax.psum_scatter(terms[2], 'tok', scatter_dimension=1, tiled=True)  109 us
    all_gather x2, waiting for transfers between devices, full_steps(): lax.all_gather(owned[0], 'tok', axis=1, tiled=True)  82.4 us
    all_gather x2, waiting for transfers between devices, full_steps(): lax.all_gather(owned[2], 'tok', axis=1, tiled=True)  59.7 us
    ppermute x8, waiting for transfers between devices, collected_by_bits(): received = lax.ppermute(blocks, axis, [(i, i ^ bit) for i in range(count)])  50.7 us
    all_gather x1, waiting for transfers between devices, shards(): lax.all_gather(fast_first, 'tok', axis=1, tiled=True)  38.8 us
    all_gather x1, waiting for transfers between devices, shards(): lax.all_gather(fast_third, 'tok', axis=1, tiled=True)  37.3 us
  transfers between devices with their start and end apart: 21, of which 18 were waited for; matrix products, arithmetic and copies ran while one was open for 8% of the time, Pallas kernels for 0%

profile of v1, /device:TPU:0, one launch (start us, length us, event | category | flops | bytes accessed | tf_op | source)
XLA Modules:
  0.0 765.5 jit_solution(2988584175845061346)
XLA Ops:
  11.3 38.8 %all-gather.8.cloned.1.call-done = bf16[2,512,512]{2,1,0:T(8,128)(2,1)} async-done(((bf16[2,32,512]{2,1,0:T(8,128)(2,1)}), bf16[2,512,512]{2,1,0:T(8,128)(2,1)}) %all-gather.8.cloned.1.call-update) | async-done | bytes 1048592 | tf_op jit(solution)/shard_map/all_gather | solution.py:96
  51.9 37.3 %all-gather.10.cloned.1.call-done = bf16[2,512,512]{2,1,0:T(8,128)(2,1)} async-done(((bf16[2,32,512]{2,1,0:T(8,128)(2,1)}), bf16[2,512,512]{2,1,0:T(8,128)(2,1)}) %all-gather.10.cloned.1.call-update) | async-done | bytes 1048592 | tf_op jit(solution)/shard_map/all_gather | solution.py:97
  90.9 1.9 fusion.34
  92.9 35.4 %all-gather.12.cloned.1.call-done = bf16[2,512,512]{2,1,0:T(8,128)(2,1)} async-done(((bf16[2,32,512]{2,1,0:T(8,128)(2,1)}), bf16[2,512,512]{2,1,0:T(8,128)(2,1)}) %all-gather.12.cloned.1.call-update) | async-done | bytes 1048592 | tf_op jit(solution)/shard_map/all_gather | solution.py:98
  130.6 1.8 fusion.35
  135.3 1.9 fusion.37
  137.3 3.2 fusion.36
  142.8 1.9 fusion.39
  144.7 3.3 fusion.38
  148.1 44.5 %reduce-scatter.7.cloned.1.call-done = f32[2,32,512]{2,1,0:T(8,128)} async-done(((f32[2,512,512]{2,1,0:T(8,128)}), f32[2,32,512]{2,1,0:T(8,128)}) %reduce-scatter.7.cloned.1.call-update) | async-done | bytes 131088 | tf_op jit(solution)/shard_map/reduce_scatter | solution.py:67
  192.7 64.3 %reduce-scatter.9.cloned.1.call-done = f32[2,32,512]{2,1,0:T(8,128)} async-done(((f32[2,512,512]{2,1,0:T(8,128)}), f32[2,32,512]{2,1,0:T(8,128)}) %reduce-scatter.9.cloned.1.call-update) | async-done | bytes 131088 | tf_op jit(solution)/shard_map/reduce_scatter | solution.py:65
  257.1 64.3 %reduce-scatter.13.cloned.1.call-done = f32[2,32,512]{2,1,0:T(8,128)} async-done(((f32[2,512,512]{2,1,0:T(8,128)}), f32[2,32,512]{2,1,0:T(8,128)}) %reduce-scatter.13.cloned.1.call-update) | async-done | bytes 131088 | tf_op jit(solution)/shard_map/reduce_scatter | solution.py:67
  321.7 64.3 %reduce-scatter.11.cloned.1.call-done = f32[2,32,512]{2,1,0:T(8,128)} async-done(((f32[2,512,512]{2,1,0:T(8,128)}), f32[2,32,512]{2,1,0:T(8,128)}) %reduce-scatter.11.cloned.1.call-update) | async-done | bytes 131088 | tf_op jit(solution)/shard_map/reduce_scatter | solution.py:66
  390.3 60.2 %reduce-scatter.17.cloned.1.call-done = f32[2,32,512]{2,1,0:T(8,128)} async-done(((f32[2,512,512]{2,1,0:T(8,128)}), f32[2,32,512]{2,1,0:T(8,128)}) %reduce-scatter.17.cloned.1.call-update) | async-done | bytes 131088 | tf_op jit(solution)/shard_map/reduce_scatter | solution.py:66
  458.4 2.0 fusion.69
  461.6 1.8 copy.82
  463.4 1.8 copy.84
  466.4 2.7 collective-permute-done.2
  477.5 56.6 %reduce-scatter.15.cloned.1.call-done = f32[2,32,512]{2,1,0:T(8,128)} async-done(((f32[2,512,512]{2,1,0:T(8,128)}), f32[2,32,512]{2,1,0:T(8,128)}) %reduce-scatter.15.cloned.1.call-update) | async-done | bytes 131088 | tf_op jit(solution)/shard_map/reduce_scatter | solution.py:65
  534.1 2.6 fusion.9
  544.0 2.0 multiply_reduce_fusion.1
  546.0 44.8 %collective-permute-done.7 = f32[8,2,32,512]{3,2,0,1:T(8,128)S(1)} collective-permute-done((f32[8,2,32,512]{3,2,0,1:T(8,128)S(1)}, f32[8,2,32,512]{3,2,0,1:T(8,128)S(1)}, u32[]{:S(2)}, u32[]{:S(2)}) %collective-permute-start.7) | collective-permute-done | bytes 1048608 | tf_op jit(solution)/shard_map/ppermute | solution.py:18
  592.7 19.5 %all-gather.14.cloned.1.call-done = f32[2,512,512]{2,1,0:T(8,128)} async-done(((f32[2,32,512]{2,1,0:T(8,128)}), f32[2,512,512]{2,1,0:T(8,128)}) %all-gather.14.cloned.1.call-update) | async-done | bytes 2097168 | tf_op jit(solution)/shard_map/all_gather | solution.py:81
  612.2 2.4 fusion
  614.6 40.0 %all-gather.16.cloned.1.call-done = f32[2,512,512]{2,1,0:T(8,128)} async-done(((f32[2,32,512]{2,1,0:T(8,128)}), f32[2,512,512]{2,1,0:T(8,128)}) %all-gather.16.cloned.1.call-update) | async-done | bytes 2097168 | tf_op jit(solution)/shard_map/all_gather | solution.py:79
  654.6 2.1 fusion.1
  656.7 40.2 %all-gather.18.cloned.1.call-done = f32[2,512,512]{2,1,0:T(8,128)} async-done(((f32[2,32,512]{2,1,0:T(8,128)}), f32[2,512,512]{2,1,0:T(8,128)}) %all-gather.18.cloned.1.call-update) | async-done | bytes 2097168 | tf_op jit(solution)/shard_map/all_gather | solution.py:81
  696.9 42.4 %all-gather.20.cloned.1.call-done = f32[2,512,512]{2,1,0:T(8,128)} async-done(((f32[2,32,512]{2,1,0:T(8,128)}), f32[2,512,512]{2,1,0:T(8,128)}) %all-gather.20.cloned.1.call-update) | async-done | bytes 2097168 | tf_op jit(solution)/shard_map/all_gather | solution.py:79
  739.3 7.5 multiply_reduce_fusion.4
  748.5 3.5 convolution_convert_fusion
  752.1 2.4 convolution_bitcast_fusion.3
  754.5 3.2 convolution_convert_fusion.1
  (135 shorter events, 51.1 us)
Async XLA Ops:
  6.5 4.2 copy-start.18
  6.5 43.6 %all-gather.8.cloned.1.call-start = ((), (), s32[]{:S(2)}) async-start(), calls=%async_computation.6 | async-start | bytes 1114112 | tf_op jit(solution)/shard_map/all_gather | solution.py:96
  7.3 81.9 %all-gather.10.cloned.1.call-start = ((), (), s32[]{:S(2)}) async-start(), calls=%async_computation.7 | async-start | bytes 1114112 | tf_op jit(solution)/shard_map/all_gather | solution.py:97
  8.0 120.2 %all-gather.12.cloned.1.call-start = ((), (), s32[]{:S(2)}) async-start(), calls=%async_computation.8 | async-start | bytes 1114112 | tf_op jit(solution)/shard_map/all_gather | solution.py:98
  8.7 2.6 copy-start.22
  8.8 183.9 %reduce-scatter.7.cloned.1.call-start = ((), (), s32[]{:S(2)}) async-start(), calls=%async_computation.9 | async-start | bytes 2228224 | tf_op jit(solution)/shard_map/reduce_scatter | solution.py:67
  51.8 78.0 %copy-start.7 = (f32[2,128,512]{2,1,0:T(8,128)}, f32[2,128,512]{2,1,0:T(8,128)S(1)}, u32[]{:S(2)}) copy-start(f32[2,128,512]{2,1,0:T(8,128)S(1)} %fusion.72) | copy-start | bytes 1572868
  92.8 164.2 %reduce-scatter.9.cloned.1.call-start = ((), (), s32[]{:S(2)}) async-start(), calls=%async_computation.11 | async-start | bytes 2228224 | tf_op jit(solution)/shard_map/reduce_scatter | solution.py:65
  132.5 188.9 %reduce-scatter.13.cloned.1.call-start = ((), (), s32[]{:S(2)}) async-start(), calls=%async_computation.14 | async-start | bytes 2228224 | tf_op jit(solution)/shard_map/reduce_scatter | solution.py:67
  137.2 3.3 copy-start.1
  137.2 248.7 %reduce-scatter.11.cloned.1.call-start = ((), (), s32[]{:S(2)}) async-start(), calls=%async_computation.13 | async-start | bytes 2228224 | tf_op jit(solution)/shard_map/reduce_scatter | solution.py:66
  140.5 2.4 copy-start.11
  140.5 310.0 %reduce-scatter.17.cloned.1.call-start = ((), (), s32[]{:S(2)}) async-start(), calls=%async_computation.18 | async-start | bytes 2228224 | tf_op jit(solution)/shard_map/reduce_scatter | solution.py:66
  140.5 2.3 copy-start.9
  144.7 389.4 %reduce-scatter.15.cloned.1.call-start = ((), (), s32[]{:S(2)}) async-start(), calls=%async_computation.16 | async-start | bytes 2228224 | tf_op jit(solution)/shard_map/reduce_scatter | solution.py:65
  148.1 464.1 %all-gather.14.cloned.1.call-start = ((), (), s32[]{:S(2)}) async-start(), calls=%async_computation.10 | async-start | bytes 2228224 | tf_op jit(solution)/shard_map/all_gather | solution.py:81
  192.7 462.0 %all-gather.16.cloned.1.call-start = ((), (), s32[]{:S(2)}) async-start(), calls=%async_computation.12 | async-start | bytes 2228224 | tf_op jit(solution)/shard_map/all_gather | solution.py:79
  257.0 439.9 %all-gather.18.cloned.1.call-start = ((), (), s32[]{:S(2)}) async-start(), calls=%async_computation.15 | async-start | bytes 2228224 | tf_op jit(solution)/shard_map/all_gather | solution.py:81
  321.4 417.9 %all-gather.20.cloned.1.call-start = ((), (), s32[]{:S(2)}) async-start(), calls=%async_computation.17 | async-start | bytes 2228224 | tf_op jit(solution)/shard_map/all_gather | solution.py:79
  385.9 1.6 collective-permute-start
  389.2 63.8 %collective-permute-start.1 = (f32[2,2,32,512]{3,2,1,0:T(8,128)}, f32[2,2,32,512]{3,2,1,0:T(8,128)}, u32[]{:S(2)}, u32[]{:S(2)}) collective-permute-start(f32[2,2,32,512]{3,2,1,0:T(8,128)} %get-tuple-element.31), channel_id=1, source_target_pairs={{0,2},{1,3},{2,0},{3,1},{4,6},{5,7},{6,4},{7,5},{8,10},{9,11},{10,... | collective-permute-start | bytes 786440 | tf_op jit(solution)/shard_map/ppermute | solution.py:18
  450.5 1.6 collective-permute-start.4
  454.8 14.3 %collective-permute-start.2 = (f32[4,2,32,512]{3,2,1,0:T(8,128)}, f32[4,2,32,512]{3,2,1,0:T(8,128)}, u32[]{:S(2)}, u32[]{:S(2)}) collective-permute-start(f32[4,2,32,512]{3,2,1,0:T(8,128)} %bitcast.15), channel_id=1, source_target_pairs={{0,4},{1,5},{2,6},{3,7},{4,0},{5,1},{6,2},{7,3},{8,12},{9,13},{10,... | collective-permute-start | bytes 1572872 | tf_op jit(solution)/shard_map/ppermute | solution.py:18
  457.0 8.4 %collective-permute-start.5 = (f32[2,2,32,512]{3,2,1,0:T(8,128)}, f32[2,2,32,512]{3,2,1,0:T(8,128)}, u32[]{:S(2)}, u32[]{:S(2)}) collective-permute-start(f32[2,2,32,512]{3,2,1,0:T(8,128)} %get-tuple-element.29), channel_id=1, source_target_pairs={{0,2},{1,3},{2,0},{3,1},{4,6},{5,7},{6,4},{7,5},{8,10},{9,11},{10,... | collective-permute-start | bytes 786440 | tf_op jit(solution)/shard_map/ppermute | solution.py:18
  472.6 68.2 %collective-permute-start.3 = (f32[8,2,32,512]{3,2,0,1:T(8,128)}, f32[8,2,32,512]{3,2,0,1:T(8,128)}, u32[]{:S(2)}, u32[]{:S(2)}) collective-permute-start(f32[8,2,32,512]{3,2,0,1:T(8,128)} %copy.43), channel_id=1, source_target_pairs={{0,8},{1,9},{2,10},{3,11},{4,12},{5,13},{6,14},{7,15},{8,0},{9,1},... | collective-permute-start | bytes 3145736 | tf_op jit(solution)/shard_map/ppermute | solution.py:18
  474.8 63.0 %collective-permute-start.6 = (f32[4,2,32,512]{3,2,1,0:T(8,128)}, f32[4,2,32,512]{3,2,1,0:T(8,128)}, u32[]{:S(2)}, u32[]{:S(2)}) collective-permute-start(f32[4,2,32,512]{3,2,1,0:T(8,128)} %bitcast.40), channel_id=1, source_target_pairs={{0,4},{1,5},{2,6},{3,7},{4,0},{5,1},{6,2},{7,3},{8,12},{9,13},{10,... | collective-permute-start | bytes 1572872 | tf_op jit(solution)/shard_map/ppermute | solution.py:18
  539.4 51.4 %collective-permute-start.7 = (f32[8,2,32,512]{3,2,0,1:T(8,128)S(1)}, f32[8,2,32,512]{3,2,0,1:T(8,128)S(1)}, u32[]{:S(2)}, u32[]{:S(2)}) collective-permute-start(f32[8,2,32,512]{3,2,0,1:T(8,128)S(1)} %copy.58), channel_id=1, source_target_pairs={{0,8},{1,9},{2,10},{3,11},{4,12},{5,13},{6,14},{7,15},{8,0},{9,1},... | collective-permute-start | bytes 3145736 | tf_op jit(solution)/shard_map/ppermute | solution.py:18
  614.6 124.7 %copy-start.23 = (f32[2]{0:T(128)S(1)}, f32[2]{0:T(128)}, u32[]{:S(2)}) copy-start(f32[2]{0:T(128)} %param.15) | copy-start | bytes 28
  739.3 7.6 copy-start.20
  752.1 2.4 copy-start.2
  752.1 2.4 copy-start.19
  754.5 3.2 copy-start.21
  (13 other events, 19.0 us)
Sparse Core Ops, SparseCore 0:
  9.5 40.5 all-gather.7
  52.3 36.8 all-gather.9
  91.4 36.8 all-gather.11
  131.8 60.7 reduce-scatter.6
  196.2 60.7 reduce-scatter.8
  260.6 60.7 reduce-scatter.12
  325.1 60.7 reduce-scatter.10
  389.7 60.7 reduce-scatter.16
  454.2 79.8 reduce-scatter.14
  536.1 75.9 all-gather.13
  614.4 40.1 all-gather.15
  656.7 40.1 all-gather.17
  699.1 40.1 all-gather.19
